TPU v7x, 256 devices: a whole 4x4x8 slice. The times are simulated.
256 devices in a mesh: dp: 4 (over x), vocab: 64 (over y, z, core).
Axes of the slice: x: 4, y: 4, z: 8, core: 2. Of those that a mesh axis runs over, the one named last changes fastest.
Arguments:
- hidden: bfloat16 [1024, 4096], P(('dp', 'vocab')), may hold values from -48 to 48
- weight: bfloat16 [65536, 4096], P('vocab'), may hold values from -3 to 3
- teacher: bfloat16 [1024, 8192], P('dp', 'vocab'), may hold values from 0 to 0.002, as said below
- block_ids: int32 [8, 64], P('dp'), may hold values from 0 to 511, as said below
Outputs:
- grad_hidden: bfloat16 [1024, 4096], P(('dp', 'vocab'))
- grad_weight: bfloat16 [65536, 4096], P('vocab', 'dp')
Inputs may be any that keep to these rules, and one draw needn't show every extreme that they name: `block_ids`: row b lists 64 different vocabulary blocks in no fixed order; frequent blocks recur over many rows. `teacher`: all entries are positive.
All inputs are finite; a program needn't handle non-finite values.
Results may differ from a plain program's by a relative error of at most 0.0051.
Values may be sent and summed in bfloat16 or wider, within the bound.
A program may use at most 128 MiB of HBM per device.

v0:
```python
import jax
import jax.numpy as jnp
from jax import lax
from jax.sharding import PartitionSpec as P

BLK = 128


loss_scale = 1024.0


def shards(hidden, weight, teacher, block_ids):
    vocab_rows = weight.shape[0]
    owned_blocks = vocab_rows // BLK
    vocab_pos = lax.axis_index("vocab")
    full_hidden = lax.all_gather(hidden, "vocab", axis=0, tiled=True)
    token_count = full_hidden.shape[0]
    logits = lax.dot_general(
        full_hidden, weight, (((1,), (1,)), ((), ())), preferred_element_type=jnp.float32
    )
    row_top = lax.pmax(jnp.max(logits, axis=1), "vocab")
    exp_terms = jnp.exp(logits - row_top[:, None])
    row_total = lax.psum(jnp.sum(exp_terms, axis=1), "vocab")
    block_count = token_count // BLK
    first_block = vocab_pos * owned_blocks
    block_range = jnp.arange(owned_blocks, dtype=jnp.int32)
    tile_cols = lax.all_gather(teacher, "vocab", axis=1, tiled=True)
    slot_count = tile_cols.shape[1] // BLK
    owned = block_ids - first_block
    onehot = (owned[:, :, None] == block_range[None, None, :]).astype(jnp.bfloat16)
    shaped = tile_cols.reshape(block_count, BLK, slot_count, BLK)
    placed = jnp.einsum("bkv,btkc->btvc", onehot, shaped, preferred_element_type=jnp.float32)
    target = placed
    row_mass = jnp.sum(tile_cols, axis=1, dtype=jnp.float32)
    target = target.reshape(token_count, vocab_rows)
    grad_logits = (
        loss_scale * (row_mass[:, None] * (exp_terms / row_total[:, None]) - target)
    ).astype(jnp.bfloat16)
    grad_hidden = lax.psum_scatter(
        jnp.dot(grad_logits, weight, preferred_element_type=jnp.float32),
        "vocab",
        scatter_dimension=0,
        tiled=True,
    ).astype(jnp.bfloat16)
    summed = lax.psum_scatter(
        lax.dot_general(
            full_hidden, grad_logits, (((0,), (0,)), ((), ())), preferred_element_type=jnp.float32
        ),
        "dp",
        scatter_dimension=0,
        tiled=True,
    )
    grad_weight = summed.T.astype(jnp.bfloat16)
    return (grad_hidden, grad_weight)


def solution(mesh):
    placed = (P(("dp", "vocab"), None), P("vocab", None), P("dp", "vocab"), P("dp", None))
    return jax.shard_map(
        shards,
        mesh=mesh,
        in_specs=placed,
        out_specs=(P(("dp", "vocab"), None), P("vocab", "dp")),
        check_vma=False,
    )
```

profile of v0, /device:TPU:1, one launch (start us, length us, event | category | flops | bytes accessed | tf_op | source)
XLA Modules:
  0.0 672.6 jit_solution(1897077753435685286)
XLA Ops:
  7.2 0.0 all-gather.6.cloned.1.call-start
  7.2 0.7 all-gather.6.cloned.1.call-update
  7.9 0.0 all-gather.4.cloned.1.call-start
  7.9 0.7 all-gather.4.cloned.1.call-update
  8.6 0.0 reduce-scatter.2.cloned.1.call-start
  8.7 0.7 broadcast_subtract_fusion
  9.4 83.1 %all-gather.6.cloned.1.call-done = bf16[64,4,4096]{2,1,0:T(4,128)(2,1)} async-done(((bf16[1,4,4096]{2,1,0:T(4,128)(2,1)}), bf16[64,4,4096]{2,1,0:T(4,128)(2,1)}) %all-gather.6.cloned.1.call-update) | async-done | bytes 2097168 | tf_op jit(solution)/shard_map/all_gather | solution.py:16
  92.5 2.5 reshape.17
  95.0 5.8 fusion.11
  100.9 124.0 %pmax.7 = f32[256]{0:T(256)S(1)} all-reduce(f32[256]{0:T(256)S(1)} %get-tuple-element.2), channel_id=1, replica_groups=mesh['dp'=4,'vocab'=64] {'vocab'}, use_global_device_ids=true, to_apply=%region_2.0 | all-reduce | flops 256 | bytes 2048 | tf_op jit(solution)/shard_map/pmax | solution.py:21
  224.9 0.3 fusion.4
  225.2 126.3 %psum.7 = f32[256]{0:T(256)S(1)} all-reduce(f32[256]{0:T(256)S(1)} %fusion.4), channel_id=1, replica_groups=mesh['dp'=4,'vocab'=64] {'vocab'}, use_global_device_ids=true, to_apply=%region_4.0 | all-reduce | flops 256 | bytes 2048 | tf_op jit(solution)/shard_map/psum | solution.py:23
  351.4 0.0 all-gather.4.cloned.1.call-done
  351.4 3.4 copy.7
  354.8 0.0 copy-start
  354.8 0.8 fusion
  355.6 1.4 copy-done
  357.0 0.0 copy-start.1
  357.0 0.7 convert_reduce_fusion
  357.7 0.3 copy-done.1
  358.0 8.5 %convolution_bitcast_fusion = f32[4096,1024]{0,1:T(8,128)} fusion(bf16[256,4096]{1,0:T(8,128)(2,1)S(1)} %reshape.17, f32[32,8,8,128]{3,2,1,0:T(8,128)S(1)} %bitcast.35, f32[256,1024]{1,0:T(8,128)S(1)} %get-tuple-element.3, f32[256]{0:T(256)S(1)} %psum.7, f32[256]{0:T(256)S(1)} %pmax.7, f32[256]{0:T(256)S(1)} %convert_reduce_fusion), kind=kOutput, calls=%fused_computation | convolution fusion | flops 2149056512 | bytes 20974592 | tf_op jit(solution)/shard_map/dot_general | solution.py:46
  366.5 0.0 copy-start.3
  366.5 0.0 copy-start.2
  366.5 0.0 reduce-scatter.2.cloned.1.call-update
  366.5 0.6 copy-done.3
  367.2 0.6 dynamic-slice
  368.4 0.0 copy-done.2
  368.4 8.0 %fusion.9 = f32[256,4096]{1,0:T(8,128)} fusion(bf16[1024,4096]{1,0:T(8,128)(2,1)} %param.5, f32[32,8,8,128]{3,2,1,0:T(8,128)S(1)} %bitcast.36, f32[256,1024]{1,0:T(8,128)S(1)} %get-tuple-element.3, f32[256]{0:T(256)S(1)} %psum.7, f32[256]{0:T(256)S(1)} %pmax.7, f32[256]{0:T(256)S(1)} %convert_reduce_fusion), kind=kOutput, calls=%fused_computation.15 | convolution fusion | flops 2149056512 | bytes 14683136 | tf_op jit(solution)/shard_map/dot_general | solution.py:40
  376.4 285.1 %all-reduce.2 = bf16[256,4096]{1,0:T(8,128)(2,1)S(1)} all-reduce(f32[256,4096]{1,0:T(8,128)} %fusion.9), channel_id=2, replica_groups=mesh['dp'=4,'vocab'=64] {'vocab'}, use_global_device_ids=true, to_apply=%region_5.0.clone | all-reduce | flops 1048576 | bytes 6291456
  661.6 0.6 dynamic-slice_convert_fusion
  662.2 0.0 reduce-scatter.2.cloned.1.call-done
  662.2 3.8 convert_bitcast_fusion
Async XLA Ops:
  7.2 85.3 %all-gather.6.cloned.1.call-start = ((), (), s32[]{:S(2)}) async-start(), calls=%async_computation.3 | async-start | bytes 2129920 | tf_op jit(solution)/shard_map/all_gather | solution.py:16
  7.9 343.5 %all-gather.4.cloned.1.call-start = ((), (), s32[]{:S(2)}) async-start(), calls=%async_computation.1 | async-start | bytes 4259840 | tf_op jit(solution)/shard_map/all_gather | solution.py:27
  8.6 653.6 %reduce-scatter.2.cloned.1.call-start = ((), (), s32[]{:S(2)}) async-start(), calls=%async_computation.2 | async-start | bytes 20971520 | tf_op jit(solution)/shard_map/reduce_scatter | solution.py:45
  354.8 2.2 copy-start
  357.0 1.0 copy-start.1
  366.5 0.7 copy-start.3
  366.5 1.9 copy-start.2
Sparse Core Ops, SparseCore 0:
  10.7 81.7 all-gather.5
  95.1 73.6 all-gather.3
  366.6 144.0 reduce-scatter.1
where the time goes:
time: 678 us; the launch traced here: 673 us
  blocking collectives  535 us (79%)
  waiting for transfers between devices  84.5 us (12%)
  matrix products  23.1 us (3%)
  between operations  14.5 us (2%)
  local copies, waits for them, and re-layouts  9.54 us (1%)
    unnamed x1, blocking collectives  285 us
    psum x1, blocking collectives, shards(): row_total = lax.psum(jnp.sum(exp_terms, axis=1), 'vocab')  126 us
    pmax x1, blocking collectives, shards(): row_top = lax.pmax(jnp.max(logits, axis=1), 'vocab')  124 us
    all_gather x1, waiting for transfers between devices, shards(): full_hidden = lax.all_gather(hidden, 'vocab', axis=0, tiled=True)  83.1 us
  transfers between devices with their start and end apart: 3, of which 1 were waited for; matrix products, arithmetic and copies ran while one was open for 3% of the time, Pallas kernels for 0%

commit v1 on v0

v1 whole, which is shorter than its diff:
```python
import jax
import jax.numpy as jnp
from jax import lax
from jax.experimental import pallas as pl
from jax.experimental.pallas import tpu as pltpu
from jax.sharding import PartitionSpec as P

BLK = 128
loss_scale = 1024.0
BF = jnp.bfloat16
F32 = jnp.float32
MESH = pl.DeviceIdType.MESH

D = 4096
V = 1024
T = 256
DC = 1024
NX, NY, NZ = 4, 4, 8


def ring(buf, n, pos, device, unit, half, ssem, rsem):
    h = n // 2

    def copy(way, step):
        sign = 1 if way == 0 else -1
        origin = lax.rem(pos - sign * (step - 1) + n, n)
        ref = unit(origin) if step < h else half(origin, way)
        return pltpu.make_async_remote_copy(
            src_ref=ref, dst_ref=ref, send_sem=ssem.at[way, step - 1],
            recv_sem=rsem.at[way, step - 1],
            device_id=device(lax.rem(pos + sign + n, n)), device_id_type=MESH)

    def arrival(way, step):
        sign = 1 if way == 0 else -1
        origin = lax.rem(pos - sign * step + n, n)
        ref = unit(origin) if step < h else half(origin, way)
        return pltpu.make_async_remote_copy(
            src_ref=ref, dst_ref=ref, send_sem=ssem.at[way, step - 1],
            recv_sem=rsem.at[way, step - 1],
            device_id=device(lax.rem(pos + sign + n, n)), device_id_type=MESH)

    def start(step):
        for way in range(2):
            copy(way, step).start()

    def arrive(step):
        for way in range(2):
            arrival(way, step).wait_recv()

    def drain():
        for step in range(1, h + 1):
            for way in range(2):
                copy(way, step).wait_send()

    return start, arrive, drain, h


def kernel(hidden_ref, weight_ref, teacher_ref, sel_ref, gh_ref, gw_ref,
           w, hraw, hid, tea, craw, hidc, rel, logits, gt, g, graw, pair, ssum, r1, s2, s2f, r2,
           st0, st1, st2s, st2, acc,
           loc_sem, hs, hr, hfs, hfr, ts, tr, tfs, tfr, xs, xr, xfs, xfr,
           s1s, s1r, s2s, s2r, gs, gr, ps, pr, r1s, r1r, r2s, r2r):
    d = lax.axis_index("dp")
    v = lax.axis_index("vocab")
    y = v // (2 * NZ)
    z = lax.rem(v // 2, NZ)
    c = lax.rem(v, 2)
    me = lax.rem(v, 2 * NZ)

    def dev(yy, zz, cc):
        return {"dp": d, "vocab": (yy * NZ + zz) * 2 + cc}

    def xdev(dd):
        return {"dp": dd, "vocab": v}

    sib = dev(y, z, 1 - c)
    dr, dl, do = lax.rem(d + 1, NX), lax.rem(d + 3, NX), lax.rem(d + 2, NX)

    def remote(src, dst, s, r, device):
        return pltpu.make_async_remote_copy(src_ref=src, dst_ref=dst, send_sem=s, recv_sem=r,
                                            device_id=device, device_id_type=MESH)

    copy_h = pltpu.make_async_copy(hidden_ref, hraw.at[y, z, c], loc_sem.at[0])
    copy_t = pltpu.make_async_copy(teacher_ref, tea.at[y, z, c], loc_sem.at[1])
    copy_w = pltpu.make_async_copy(weight_ref, w, loc_sem.at[2])
    copy_h.start()
    copy_t.start()
    copy_w.start()

    barrier = pltpu.get_barrier_semaphore()
    for k in range(1, 16):
        p = lax.rem(me + k, 16)
        pl.semaphore_signal(barrier, inc=1, device_id=dev(y, p // 2, lax.rem(p, 2)),
                            device_id_type=MESH)
    for k in range(1, NY):
        pl.semaphore_signal(barrier, inc=1, device_id=dev(lax.rem(y + k, NY), z, c),
                            device_id_type=MESH)
    for dd in (dr, dl):
        pl.semaphore_signal(barrier, inc=1, device_id=xdev(dd), device_id_type=MESH)
    pl.semaphore_wait(barrier, 20)

    def gather(buf, half_of, ssem, rsem, fss, frs):
        def build(cc):
            def y_first(o):
                return buf.at[o, z, cc]

            def z_first(o):
                return buf.at[y, o, cc]

            if cc == 0:
                one = ring(buf, NY, y, lambda o: dev(o, z, cc), y_first,
                           lambda o, way: half_of(buf.at[o, z, cc], way),
                           ssem.at[0], rsem.at[0])
                unit = lambda o: buf.at[:, o, cc]
                two = ring(buf, NZ, z, lambda o: dev(y, o, cc), unit,
                           lambda o, way: buf.at[pl.ds(2 * way, 2), o, cc],
                           ssem.at[1], rsem.at[1])
                pos, n = z, NZ
            else:
                one = ring(buf, NZ, z, lambda o: dev(y, o, cc), z_first,
                           lambda o, way: half_of(buf.at[y, o, cc], way),
                           ssem.at[0], rsem.at[0])
                unit = lambda o: buf.at[o, :, cc]
                two = ring(buf, NY, y, lambda o: dev(o, z, cc), unit,
                           lambda o, way: buf.at[o, pl.ds(4 * way, 4), cc],
                           ssem.at[1], rsem.at[1])
                pos, n = y, NY

            def forward(k):
                o = lax.rem(pos + k, n)
                return remote(unit(o), unit(o), fss.at[k], frs.at[k], sib)

            steps = []
            h1, h2 = one[3], two[3]

            def first():
                one[0](1)

            steps.append(first)
            for s in range(2, h1 + 1):
                def mid(s=s):
                    one[1](s - 1)
                    one[0](s)
                steps.append(mid)

            def join():
                one[1](h1)
                two[0](1)
                forward(0).start()

            steps.append(join)
            for s in range(2, h2 + 1):
                def mid2(s=s):
                    two[1](s - 1)
                    two[0](s)
                    forward(s - 1).start()
                    forward(n - s + 1).start()
                steps.append(mid2)

            def last():
                two[1](h2)
                forward(h2).start()

            steps.append(last)

            def drain():
                one[2]()
                two[2]()
                for k in range(n):
                    forward(k).wait_send()

            def from_sibling():
                for k in range(n):
                    o = lax.rem(pos + k, n)
                    remote(unit(o), unit(o), fss.at[k], frs.at[k], sib).wait_recv()

            return steps, drain, from_sibling

        a, b = build(0), build(1)

        def both(fa, fb):
            def run():
                pl.when(c == 0)(fa)
                pl.when(c == 1)(fb)
            return run

        steps = [both(fa, fb) for fa, fb in zip(a[0], b[0])]
        return steps, both(a[1], b[1]), both(b[2], a[2])

    h_steps, h_drain, h_sib = gather(
        hraw, lambda ref, way: ref.at[:, pl.ds(way * (D // 2), D // 2)], hs, hr, hfs, hfr)
    t_steps, t_drain, t_sib = gather(tea, lambda ref, way: ref.at[way], ts, tr, tfs, tfr)

    copy_h.wait()
    for step in h_steps[:-1]:
        step()
    copy_t.wait()
    t_steps[0]()
    h_steps[-1]()

    def cols(dd):
        return pl.ds(pl.multiple_of(dd * DC, DC), DC)

    x_sends = [
        remote(hraw.at[0:2, :, c, :, cols(do)], rel.at[0], xs.at[0], xr.at[0], xdev(dr)),
        remote(hraw.at[2:4, :, c, :, cols(do)], rel.at[1], xs.at[1], xr.at[1], xdev(dl)),
        remote(hraw.at[:, :, c, :, cols(dr)], craw.at[d, :, :, c], xs.at[2], xr.at[2], xdev(dr)),
        remote(hraw.at[:, :, c, :, cols(dl)], craw.at[d, :, :, c], xs.at[3], xr.at[3], xdev(dl)),
    ]
    for copy in x_sends:
        copy.start()
    x_relays = [
        remote(rel.at[0], craw.at[dl, 0:2, :, c], xs.at[4], xr.at[4], xdev(dr)),
        remote(rel.at[1], craw.at[dr, 2:4, :, c], xs.at[5], xr.at[5], xdev(dl)),
    ]

    t_steps[1]()
    h_sib()

    def flatten(i, _):
        yy, zz = i // 4, lax.rem(i, 4)
        hid[pl.ds(pl.multiple_of(16 * i, 16), 16), :] = hraw[yy, pl.ds(2 * zz, 2)].reshape(16, D)
        return 0

    lax.fori_loop(0, 16, flatten, 0)
    t_steps[2]()

    copy_w.wait()
    top = jnp.full((1, T), -jnp.inf, F32)
    for q in range(4):
        rows = pl.ds(256 * q, 256)
        part = lax.dot_general(w[rows, :], hid[...], (((1,), (1,)), ((), ())),
                               preferred_element_type=F32)
        logits[rows, :] = part
        top = jnp.maximum(top, jnp.max(part, axis=0, keepdims=True))
        if q == 1:
            t_steps[3]()
    total = jnp.zeros((1, T), F32)
    for q in range(4):
        rows = pl.ds(256 * q, 256)
        total = total + jnp.sum(jnp.exp(logits[rows, :] - top), axis=0, keepdims=True)
    mass = lax.dot_general(jnp.ones((8, BLK), BF), tea[y, z, c].reshape(T, BLK),
                           (((1,), (1,)), ((), ())), preferred_element_type=F32)[0:1]
    st0[0:1, :] = top
    st0[1:2, :] = total
    st0[2:3, :] = mass
    st0[3:4, :] = mass
    for k in range(1, 16):
        p = lax.rem(me + k, 16)
        remote(st0, st1.at[me], s1s.at[k], s1r.at[me], dev(y, p // 2, lax.rem(p, 2))).start()
    t_steps[4]()
    for k in range(1, 16):
        p = lax.rem(me + k, 16)
        remote(st0, st1.at[p], s1s.at[k], s1r.at[p], dev(y, p // 2, lax.rem(p, 2))).wait_recv()

    def merge(parts):
        m = parts[0][0:1]
        for part in parts[1:]:
            m = jnp.maximum(m, part[0:1])
        s = jnp.zeros((1, T), F32)
        a = jnp.zeros((1, T), F32)
        for part in parts:
            s = s + part[1:2] * jnp.exp(part[0:1] - m)
            a = a + part[2:3]
        return m, s, a

    m1, s1, a1 = merge([st0[...]] + [st1[lax.rem(me + k, 16)] for k in range(1, 16)])
    st2s[0:1, :] = m1
    st2s[1:2, :] = s1
    st2s[2:3, :] = a1
    st2s[3:4, :] = a1
    for k in range(1, NY):
        p = lax.rem(y + k, NY)
        remote(st2s, st2.at[y], s2s.at[k], s2r.at[y], dev(p, z, c)).start()
    t_steps[5]()
    for k in range(1, NY):
        p = lax.rem(y + k, NY)
        remote(st2s, st2.at[p], s2s.at[k], s2r.at[p], dev(p, z, c)).wait_recv()
    m2, s2_, a2 = merge([st2s[...]] + [st2[lax.rem(y + k, NY)] for k in range(1, NY)])
    scale = loss_scale * a2 / s2_

    x_sends[0].wait_recv()
    x_relays[0].start()
    x_sends[1].wait_recv()
    x_relays[1].start()
    t_steps[6]()
    t_sib()

    def grads(j, _):
        rows = pl.ds(pl.multiple_of(j * BLK, BLK), BLK)
        for tb in range(2):
            k = sel_ref[tb * 8 + j]
            found = jnp.where(k >= 0, loss_scale, 0.0)
            kk = jnp.maximum(k, 0)
            tile = tea[kk // 16, lax.rem(kk // 2, NZ), lax.rem(kk, 2), tb]
            part = slice(tb * BLK, tb * BLK + BLK)
            value = (scale[:, part] * jnp.exp(logits[rows, part] - m2[:, part])
                     - found * tile.astype(F32).T)
            gt[d, rows, part] = value.astype(BF)
        return 0

    lax.fori_loop(0, 8, grads, 0)

    def chunk(dd, q):
        return gt.at[dd, pl.ds(256 * q, 256)]

    g_own = []
    for i in range(4):
        for way, q, to in ((0, i, dr), (1, (i + 2) % 4, dl)):
            copy = remote(chunk(d, q), chunk(d, q), gs.at[way, i], gr.at[way, i], xdev(to))
            copy.start()
            g_own.append(copy)

    def g_arrived(way, i):
        q, origin = ((i, dl), ((i + 2) % 4, dr))[way]
        to = (dr, dl)[way]
        remote(chunk(origin, q), chunk(origin, q), gs.at[way, i], gr.at[way, i],
               xdev(to)).wait_recv()

    def g_relay(way, i):
        q, origin = ((i, dl), ((i + 2) % 4, dr))[way]
        to = (dr, dl)[way]
        return remote(chunk(origin, q), chunk(origin, q), gs.at[way, 4 + i], gr.at[way, 4 + i],
                      xdev(to))

    g[...] = gt[d].T

    def back(i, _):
        span = pl.ds(pl.multiple_of(i * 512, 512), 512)
        part = jnp.dot(g[...], w[:, span], preferred_element_type=F32)
        graw[:, :, :, :, span] = part.reshape(NY, NZ, 2, 4, 512).astype(BF)
        return 0

    lax.fori_loop(0, 8, back, 0)

    swap = remote(graw.at[:, :, 1 - c], pair, ps.at[0], pr.at[0], sib)
    swap.start()
    for i in range(2):
        for way in range(2):
            g_arrived(way, i)
            g_relay(way, i).start()
    swap.wait_recv()

    def add_pair(i, _):
        yy, zz = i // NZ, lax.rem(i, NZ)
        ssum[yy, zz] = (graw[yy, zz, c].astype(F32) + pair[yy, zz].astype(F32)).astype(BF)
        return 0

    lax.fori_loop(0, 32, add_pair, 0)

    def reduce_steps(cc):
        if cc == 0:
            n1, p1, n2, p2 = NZ, z, NY, y
            piece = lambda o: ssum.at[:, o]
            own = lambda o: graw[o, z, cc].astype(F32) + pair[o, z].astype(F32)
            dev1, dev2 = (lambda o: dev(y, o, cc)), (lambda o: dev(o, z, cc))
        else:
            n1, p1, n2, p2 = NY, y, NZ, z
            piece = lambda o: ssum.at[o]
            own = lambda o: graw[y, o, cc].astype(F32) + pair[y, o].astype(F32)
            dev1, dev2 = (lambda o: dev(o, z, cc)), (lambda o: dev(y, o, cc))

        def slot(o):
            return r1.at[pl.ds(o * n2, n2)]

        def one(k):
            o = lax.rem(p1 + k, n1)
            return remote(piece(o), slot(p1), r1s.at[k], r1r.at[p1], dev1(o))

        def one_in(k):
            o = lax.rem(p1 + k, n1)
            return remote(piece(o), slot(o), r1s.at[k], r1r.at[o], dev1(o))

        def two(k):
            o = lax.rem(p2 + k, n2)
            return remote(s2.at[o], r2.at[p2], r2s.at[k], r2r.at[p2], dev2(o))

        def two_in(k):
            o = lax.rem(p2 + k, n2)
            return remote(s2.at[o], r2.at[o], r2s.at[k], r2r.at[o], dev2(o))

        def start():
            for k in range(1, n1):
                one(k).start()

        def middle():
            for k in range(1, n1):
                one_in(k).wait_recv()

            def add(i, _):
                total = own(i)
                for k in range(1, n1):
                    total = total + r1[lax.rem(p1 + k, n1) * n2 + i].astype(F32)
                s2f[i] = total
                s2[i] = total.astype(BF)
                return 0

            lax.fori_loop(0, n2, add, 0)
            for k in range(1, n2):
                two(k).start()

        def finish():
            for k in range(1, n2):
                two_in(k).wait_recv()
            total = s2f[p2]
            for k in range(1, n2):
                total = total + r2[lax.rem(p2 + k, n2)].astype(F32)
            gh_ref[...] = total.astype(BF)
            for k in range(1, n1):
                one(k).wait_send()
            for k in range(1, n2):
                two(k).wait_send()

        return start, middle, finish

    ra, rb = reduce_steps(0), reduce_steps(1)

    def phase(i):
        pl.when(c == 0)(ra[i])
        pl.when(c == 1)(rb[i])

    phase(0)

    x_sends[2].wait_recv()
    x_sends[3].wait_recv()
    x_relays[0].wait_recv()
    x_relays[1].wait_recv()
    x_fwd = [remote(craw.at[dd, :, :, c], craw.at[dd, :, :, c], xfs.at[i], xfr.at[i], sib)
             for i, dd in enumerate((dl, dr, do))]
    for copy in x_fwd:
        copy.start()
    for i, dd in enumerate((dl, dr, do)):
        remote(craw.at[dd, :, :, 1 - c], craw.at[dd, :, :, 1 - c], xfs.at[i], xfr.at[i],
               sib).wait_recv()
    for dd in (dl, dr, do):
        def flatten_cols(i, _, dd=dd):
            yy, zz = i // 4, lax.rem(i, 4)
            hidc[dd, pl.ds(pl.multiple_of(16 * i, 16), 16), :] = (
                craw[dd, yy, pl.ds(2 * zz, 2)].reshape(16, DC))
            return 0

        lax.fori_loop(0, 16, flatten_cols, 0)
    hidc[d] = hid[:, cols(d)]

    for i in range(2, 4):
        for way in range(2):
            g_arrived(way, i)

    def near(q, _):
        rows = pl.ds(pl.multiple_of(q * 256, 256), 256)
        part = jnp.dot(gt[d, rows], hidc[d], preferred_element_type=F32)
        part = part + jnp.dot(gt[dl, rows], hidc[dl], preferred_element_type=F32)
        part = part + jnp.dot(gt[dr, rows], hidc[dr], preferred_element_type=F32)
        acc[rows, :] = part
        return 0

    lax.fori_loop(0, 4, near, 0)
    phase(1)

    for i in range(2):
        for way, q in ((0, i), (1, (i + 2) % 4)):
            remote(chunk(do, q), chunk(do, q), gs.at[way, 4 + i], gr.at[way, 4 + i],
                   xdev((dr, dl)[way])).wait_recv()

    def far(q, _):
        rows = pl.ds(pl.multiple_of(q * 256, 256), 256)
        part = jnp.dot(gt[do, rows], hidc[do], preferred_element_type=F32)
        gw_ref[rows, :] = (acc[rows, :] + part).astype(BF)
        return 0

    lax.fori_loop(0, 4, far, 0)
    phase(2)

    h_drain()
    t_drain()
    for copy in x_sends + x_relays + x_fwd + g_own + [swap]:
        copy.wait_send()
    for i in range(2):
        for way in range(2):
            g_relay(way, i).wait_send()
    for k in range(1, 16):
        p = lax.rem(me + k, 16)
        remote(st0, st1.at[me], s1s.at[k], s1r.at[me], dev(y, p // 2, lax.rem(p, 2))).wait_send()
    for k in range(1, NY):
        p = lax.rem(y + k, NY)
        remote(st2s, st2.at[y], s2s.at[k], s2r.at[y], dev(p, z, c)).wait_send()


def shards(hidden, weight, teacher, block_ids):
    first = lax.axis_index("vocab") * (V // BLK)
    owned = first + jnp.arange(V // BLK, dtype=jnp.int32)
    slots = jnp.arange(block_ids.shape[1], dtype=jnp.int32)
    sel = jnp.max(jnp.where(block_ids[:, None, :] == owned[None, :, None], slots, -1), axis=2)
    vm = pltpu.VMEM
    dma = pltpu.SemaphoreType.DMA
    return pl.pallas_call(
        kernel,
        out_shape=(jax.ShapeDtypeStruct((4, D), BF), jax.ShapeDtypeStruct((V, DC), BF)),
        in_specs=[pl.BlockSpec(memory_space=pl.ANY)] * 3
        + [pl.BlockSpec(memory_space=pltpu.SMEM)],
        out_specs=(pl.BlockSpec(memory_space=vm), pl.BlockSpec(memory_space=vm)),
        scratch_shapes=[
            vm((V, D), BF),
            vm((NY, NZ, 2, 4, D), BF),
            vm((T, D), BF),
            vm((NY, NZ, 2, 2, BLK, BLK), BF),
            vm((NX, NY, NZ, 2, 4, DC), BF),
            vm((NX, T, DC), BF),
            vm((2, 2, NZ, 4, DC), BF),
            vm((V, T), F32),
            vm((NX, V, T), BF),
            vm((T, V), BF),
            vm((NY, NZ, 2, 4, D), BF),
            vm((NY, NZ, 4, D), BF),
            vm((NY, NZ, 4, D), BF),
            vm((32, 4, D), BF),
            vm((8, 4, D), BF),
            vm((8, 4, D), F32),
            vm((8, 4, D), BF),
            vm((4, T), F32),
            vm((16, 4, T), F32),
            vm((4, T), F32),
            vm((NY, 4, T), F32),
            vm((V, DC), F32),
            dma((3,)),
            dma((2, 2, 4)), dma((2, 2, 4)), dma((8,)), dma((8,)),
            dma((2, 2, 4)), dma((2, 2, 4)), dma((8,)), dma((8,)),
            dma((6,)), dma((6,)), dma((3,)), dma((3,)),
            dma((16,)), dma((16,)), dma((4,)), dma((4,)),
            dma((2, 6)), dma((2, 6)), dma((1,)), dma((1,)),
            dma((8,)), dma((8,)), dma((8,)), dma((8,)),
        ],
        compiler_params=pltpu.CompilerParams(
            collective_id=0, has_side_effects=True, vmem_limit_bytes=60 << 20),
    )(hidden, weight, teacher.reshape(2, BLK, BLK), sel.reshape(-1))


def solution(mesh):
    placed = (P(("dp", "vocab"), None), P("vocab", None), P("dp", "vocab"), P("dp", None))
    return jax.shard_map(
        shards,
        mesh=mesh,
        in_specs=placed,
        out_specs=(P(("dp", "vocab"), None), P("vocab", "dp")),
        check_vma=False,
    )
```

time: 678 us -> 103 us (0.15)
  the two profiles are of different devices: /device:TPU:1 before, /device:TPU:64 now
where the time goes in v1:
time: 103 us; the launch traced here: 102 us
  Pallas kernels  95.8 us (93%)
  local copies, waits for them, and re-layouts  5.06 us (5%)
    pallas_call x1, Pallas kernels, shards(): pl.pallas_call(kernel, out_shape=(jax.ShapeDtypeStruct((4, D), BF), jax.S...  95.8 us
    unnamed x2, local copies, waits for them, and re-layouts  4.46 us

profile of v1, /device:TPU:64, one launch (start us, length us, event | category | flops | bytes accessed | tf_op | source)
XLA Modules:
  0.0 102.4 jit_solution(2321934515952517520)
XLA Ops:
  0.6 0.9 select_reduce_fusion
  1.5 0.6 reshape.16.sel_ref
  2.1 95.8 %shard_map.59 = (bf16[4,4096]{1,0:T(4,128)(2,1)}, bf16[1024,1024]{1,0:T(8,128)(2,1)}) custom-call(bf16[4,4096]{1,0:T(4,128)(2,1)} %hidden_ref.1, bf16[1024,4096]{1,0:T(8,128)(2,1)} %weight_ref.1, bf16[2,128,128]{2,1,0:T(8,128)(2,1)} %bitcast.1, s32[16]{0:T(128)} %reshape.16.sel_ref), custom_call_target="tpu_custom_call" | custom-call | tf_op jit(solution)/shard_map/pallas_call | solution.py:496
  97.9 1.4 %copy.8 = bf16[4,4096]{1,0:T(4,128)(2,1)} copy(bf16[4,4096]{1,0:T(4,128)(2,1)} %get-tuple-element.4) | data formatting | bytes 65536
  99.3 3.1 %copy.9 = bf16[1024,1024]{1,0:T(8,128)(2,1)} copy(bf16[1024,1024]{1,0:T(8,128)(2,1)} %get-tuple-element.5) | data formatting | bytes 4194304
  (1 shorter events, 0.0 us)

commit v2 on v1

v2 whole, which is shorter than its diff:
```python
import jax
import jax.numpy as jnp
from jax import lax
from jax.experimental import pallas as pl
from jax.experimental.pallas import tpu as pltpu
from jax.sharding import PartitionSpec as P

BLK = 128
loss_scale = 1024.0
BF = jnp.bfloat16
F32 = jnp.float32
MESH = pl.DeviceIdType.MESH

D = 4096
V = 1024
T = 256
DC = 1024
NX, NY, NZ = 4, 4, 8


def kernel(hidden_ref, weight_ref, teacher_ref, ids_ref, gh_ref, gw_ref,
           w, hraw, hid, tea, craw, hidc, rel, logits, gt, g, graw, pair, ssum, r1, s2, s2f, r2,
           st0, st1, st2s, st2, acc, sel_ref,
           loc_sem, hs, hr, hs2, hr2, hfs, hfr, ts, tr, ts2, tr2, tfs, tfr, xs, xr, xfs, xfr,
           s1s, s1r, s2s, s2r, gs, gr, ps, pr, r1s, r1r, r2s, r2r):
    d = lax.axis_index("dp")
    v = lax.axis_index("vocab")
    y = v // (2 * NZ)
    z = lax.rem(v // 2, NZ)
    c = lax.rem(v, 2)
    me = lax.rem(v, 2 * NZ)

    def dev(yy, zz, cc):
        return {"dp": d, "vocab": (yy * NZ + zz) * 2 + cc}

    def xdev(dd):
        return {"dp": dd, "vocab": v}

    sib = dev(y, z, 1 - c)
    dr, dl, do = lax.rem(d + 1, NX), lax.rem(d + 3, NX), lax.rem(d + 2, NX)

    def remote(src, dst, s, r, device):
        return pltpu.make_async_remote_copy(src_ref=src, dst_ref=dst, send_sem=s, recv_sem=r,
                                            device_id=device, device_id_type=MESH)

    copy_h = pltpu.make_async_copy(hidden_ref, hraw.at[y, z, c], loc_sem.at[0])
    copy_t = pltpu.make_async_copy(teacher_ref, tea.at[y, z, c], loc_sem.at[1])
    copy_w = pltpu.make_async_copy(weight_ref, w, loc_sem.at[2])
    copy_h.start()
    copy_t.start()
    copy_w.start()

    barrier = pltpu.get_barrier_semaphore()
    for k in range(1, 16):
        p = lax.rem(me + k, 16)
        pl.semaphore_signal(barrier, inc=1, device_id=dev(y, p // 2, lax.rem(p, 2)),
                            device_id_type=MESH)
    for k in range(1, NY):
        pl.semaphore_signal(barrier, inc=1, device_id=dev(lax.rem(y + k, NY), z, c),
                            device_id_type=MESH)
    for dd in (dr, dl):
        pl.semaphore_signal(barrier, inc=1, device_id=xdev(dd), device_id_type=MESH)
    def find(k, slots):
        out = []
        for tb in range(2):
            entry = ids_ref[tb, k] - v * (V // BLK)
            for j in range(V // BLK):
                out.append(jnp.where(entry == j, k, slots[tb * 8 + j]))
        return tuple(out)

    for i, slot in enumerate(lax.fori_loop(0, 64, find, (jnp.int32(-1),) * 16)):
        sel_ref[i] = slot
    pl.semaphore_wait(barrier, 20)

    def gather(buf, half, ss1, sr1, ss2, sr2, fss, frs):
        def build(cc):
            if cc == 0:
                n1, p1, n2, p2 = NY, y, NZ, z
                at = lambda a, b: buf.at[a, b, cc]
                dev1, dev2 = (lambda a: dev(a, z, cc)), (lambda b: dev(y, b, cc))
            else:
                n1, p1, n2, p2 = NZ, z, NY, y
                at = lambda a, b: buf.at[b, a, cc]
                dev1, dev2 = (lambda a: dev(y, a, cc)), (lambda b: dev(b, z, cc))
            h1, h2 = n1 // 2, n2 // 2

            def one(way, s, come):
                sign = 1 - 2 * way
                ref = at(lax.rem(p1 - sign * (s - 1 + come) + n1, n1), p2)
                if s == h1:
                    ref = half(ref, way)
                return remote(ref, ref, ss1.at[way, s - 1], sr1.at[way, s - 1],
                              dev1(lax.rem(p1 + sign + n1, n1)))

            def two(j, way, s, come):
                sign = 1 - 2 * way
                ref = at(lax.rem(p1 + j + n1, n1), lax.rem(p2 - sign * (s - 1 + come) + n2, n2))
                if s == h2:
                    ref = half(ref, way)
                i = ((j % n1) * 2 + way) * h2 + s - 1
                return remote(ref, ref, ss2.at[i], sr2.at[i], dev2(lax.rem(p2 + sign + n2, n2)))

            offsets = [0] + [sign * k for k in range(1, h1) for sign in (-1, 1)] + [h1]

            def spread(j):
                for way in range(2):
                    two(j, way, 1, 0).start()

            def wave(w):
                if w == 0:
                    for way in range(2):
                        one(way, 1, 0).start()
                    spread(0)
                elif w <= h1:
                    for way in range(2):
                        one(way, w, 1).wait_recv()
                        if w < h1:
                            one(way, w + 1, 0).start()
                            spread(-w if way == 0 else w)
                    if w == h1:
                        spread(h1)
                for j in reversed(offsets):
                    s = w - abs(j)
                    if 1 <= s <= h2:
                        for way in range(2):
                            two(j, way, s, 1).wait_recv()
                            if s < h2:
                                two(j, way, s + 1, 0).start()

            def drain():
                for way in range(2):
                    for s in range(1, h1 + 1):
                        one(way, s, 0).wait_send()
                    for j in offsets:
                        for s in range(1, h2 + 1):
                            two(j, way, s, 0).wait_send()

            return wave, drain

        (wave_a, drain_a), (wave_b, drain_b) = build(0), build(1)

        def forward(k, cc):
            unit = buf.at[:, lax.rem(z + k, NZ), cc]
            return remote(unit, unit, fss.at[k], frs.at[k], sib)

        def wave(w):
            pl.when(c == 0)(lambda: wave_a(w))
            pl.when(c == 1)(lambda: wave_b(w))
            if w >= 2:
                for k in sorted({w - 2, (NZ - w + 2) % NZ}):
                    forward(k, c).start()

        def drain():
            pl.when(c == 0)(drain_a)
            pl.when(c == 1)(drain_b)
            for k in range(NZ):
                forward(k, c).wait_send()

        def from_sibling():
            for k in range(NZ):
                forward(k, 1 - c).wait_recv()

        return wave, drain, from_sibling

    h_wave, h_drain, h_sib = gather(
        hraw, lambda ref, way: ref.at[:, pl.ds(way * (D // 2), D // 2)],
        hs, hr, hs2, hr2, hfs, hfr)
    t_wave, t_drain, t_sib = gather(
        tea, lambda ref, way: ref.at[way], ts, tr, ts2, tr2, tfs, tfr)
    copy_h.wait()
    copy_t.wait()
    for i in range(7):
        h_wave(i)
        if 3 <= i < 6:
            t_wave(i - 3)
    def cols(dd):
        return pl.ds(pl.multiple_of(dd * DC, DC), DC)

    x_sends = [
        remote(hraw.at[0:2, :, c, :, cols(do)], rel.at[0], xs.at[0], xr.at[0], xdev(dr)),
        remote(hraw.at[2:4, :, c, :, cols(do)], rel.at[1], xs.at[1], xr.at[1], xdev(dl)),
        remote(hraw.at[:, :, c, :, cols(dr)], craw.at[d, :, :, c], xs.at[2], xr.at[2], xdev(dr)),
        remote(hraw.at[:, :, c, :, cols(dl)], craw.at[d, :, :, c], xs.at[3], xr.at[3], xdev(dl)),
    ]
    for copy in x_sends:
        copy.start()
    x_relays = [
        remote(rel.at[0], craw.at[dl, 0:2, :, c], xs.at[4], xr.at[4], xdev(dr)),
        remote(rel.at[1], craw.at[dr, 2:4, :, c], xs.at[5], xr.at[5], xdev(dl)),
    ]
    t_wave(3)
    h_sib()

    def flatten(i, _):
        yy, zz = i // 4, lax.rem(i, 4)
        hid[pl.ds(pl.multiple_of(16 * i, 16), 16), :] = hraw[yy, pl.ds(2 * zz, 2)].reshape(16, D)
        return 0

    lax.fori_loop(0, 16, flatten, 0)
    copy_w.wait()
    top = jnp.full((1, T), -jnp.inf, F32)
    for q in range(4):
        rows = pl.ds(256 * q, 256)
        part = lax.dot_general(w[rows, :], hid[...], (((1,), (1,)), ((), ())),
                               preferred_element_type=F32)
        logits[rows, :] = part
        top = jnp.maximum(top, jnp.max(part, axis=0, keepdims=True))
        if q == 0:
            t_wave(4)
        if q == 2:
            t_wave(5)
    total = jnp.zeros((1, T), F32)
    for q in range(4):
        rows = pl.ds(256 * q, 256)
        total = total + jnp.sum(jnp.exp(logits[rows, :] - top), axis=0, keepdims=True)
    mass = lax.dot_general(jnp.ones((8, BLK), BF), tea[y, z, c].reshape(T, BLK),
                           (((1,), (1,)), ((), ())), preferred_element_type=F32)[0:1]
    st0[0:1, :] = top
    st0[1:2, :] = total
    st0[2:3, :] = mass
    st0[3:4, :] = mass
    for k in range(1, 16):
        p = lax.rem(me + k, 16)
        remote(st0, st1.at[me], s1s.at[k], s1r.at[me], dev(y, p // 2, lax.rem(p, 2))).start()
    t_wave(6)
    for k in range(1, 16):
        p = lax.rem(me + k, 16)
        remote(st0, st1.at[p], s1s.at[k], s1r.at[p], dev(y, p // 2, lax.rem(p, 2))).wait_recv()

    def merge(parts):
        m = parts[0][0:1]
        for part in parts[1:]:
            m = jnp.maximum(m, part[0:1])
        s = jnp.zeros((1, T), F32)
        a = jnp.zeros((1, T), F32)
        for part in parts:
            s = s + part[1:2] * jnp.exp(part[0:1] - m)
            a = a + part[2:3]
        return m, s, a

    m1, s1, a1 = merge([st0[...]] + [st1[lax.rem(me + k, 16)] for k in range(1, 16)])
    st2s[0:1, :] = m1
    st2s[1:2, :] = s1
    st2s[2:3, :] = a1
    st2s[3:4, :] = a1
    for k in range(1, NY):
        p = lax.rem(y + k, NY)
        remote(st2s, st2.at[y], s2s.at[k], s2r.at[y], dev(p, z, c)).start()
    x_sends[0].wait_recv()
    x_relays[0].start()
    x_sends[1].wait_recv()
    x_relays[1].start()
    for k in range(1, NY):
        p = lax.rem(y + k, NY)
        remote(st2s, st2.at[p], s2s.at[k], s2r.at[p], dev(p, z, c)).wait_recv()
    m2, s2_, a2 = merge([st2s[...]] + [st2[lax.rem(y + k, NY)] for k in range(1, NY)])
    scale = loss_scale * a2 / s2_
    t_sib()

    def grads(j, _):
        rows = pl.ds(pl.multiple_of(j * BLK, BLK), BLK)
        for tb in range(2):
            k = sel_ref[tb * 8 + j]
            found = jnp.where(k >= 0, loss_scale, 0.0)
            kk = jnp.maximum(k, 0)
            tile = tea[kk // 16, lax.rem(kk // 2, NZ), lax.rem(kk, 2), tb]
            part = slice(tb * BLK, tb * BLK + BLK)
            value = (scale[:, part] * jnp.exp(logits[rows, part] - m2[:, part])
                     - found * tile.astype(F32).T)
            gt[d, rows, part] = value.astype(BF)
        return 0

    lax.fori_loop(0, 8, grads, 0)

    def chunk(dd, q):
        return gt.at[dd, pl.ds(256 * q, 256)]
    g_own = []
    for i in range(4):
        for way, q, to in ((0, i, dr), (1, (i + 2) % 4, dl)):
            copy = remote(chunk(d, q), chunk(d, q), gs.at[way, i], gr.at[way, i], xdev(to))
            copy.start()
            g_own.append(copy)

    def g_arrived(way, i):
        q, origin = ((i, dl), ((i + 2) % 4, dr))[way]
        to = (dr, dl)[way]
        remote(chunk(origin, q), chunk(origin, q), gs.at[way, i], gr.at[way, i],
               xdev(to)).wait_recv()

    def g_relay(way, i):
        q, origin = ((i, dl), ((i + 2) % 4, dr))[way]
        to = (dr, dl)[way]
        return remote(chunk(origin, q), chunk(origin, q), gs.at[way, 4 + i], gr.at[way, 4 + i],
                      xdev(to))
    g[...] = gt[d].T
    H = D // 2

    def part_of(half):
        return pl.ds(half * H, H)

    swap = [remote(graw.at[:, :, 1 - c, :, part_of(half)], pair.at[:, :, :, part_of(half)],
                   ps.at[half], pr.at[half], sib) for half in range(2)]

    for half in range(2):
        def back(i, _):
            span = pl.ds(pl.multiple_of(i * 512, 512), 512)
            value = jnp.dot(g[...], w[:, span], preferred_element_type=F32)
            graw[:, :, :, :, span] = value.reshape(NY, NZ, 2, 4, 512).astype(BF)
            return 0

        lax.fori_loop(half * 4, half * 4 + 4, back, 0)
        swap[half].start()

    def reducer(half, z_first):
        span = part_of(half)
        if z_first:
            n1, p1, n2, p2 = NZ, z, NY, y
            piece = lambda o: ssum.at[:, o, :, span]
            own = lambda o: (graw[o, z, c, :, span].astype(F32) + pair[o, z, :, span].astype(F32))
            dev1, dev2 = (lambda o: dev(y, o, c)), (lambda o: dev(o, z, c))
        else:
            n1, p1, n2, p2 = NY, y, NZ, z
            piece = lambda o: ssum.at[o, :, :, span]
            own = lambda o: (graw[y, o, c, :, span].astype(F32) + pair[y, o, :, span].astype(F32))
            dev1, dev2 = (lambda o: dev(o, z, c)), (lambda o: dev(y, o, c))

        def one(k, come):
            o = lax.rem(p1 + k, n1)
            to = o if come else p1
            return remote(piece(o), r1.at[pl.ds(to * n2, n2), :, span], r1s.at[half, k],
                          r1r.at[half, to], dev1(o))

        def two(k, come):
            o = lax.rem(p2 + k, n2)
            to = o if come else p2
            return remote(s2.at[o, :, span], r2.at[to, :, span], r2s.at[half, k],
                          r2r.at[half, to], dev2(o))

        def start():
            for k in range(1, n1):
                one(k, False).start()

        def middle():
            for k in range(1, n1):
                one(k, True).wait_recv()

            def add(i, _):
                value = own(i)
                for k in range(1, n1):
                    value = value + r1[lax.rem(p1 + k, n1) * n2 + i, :, span].astype(F32)
                s2f[i, :, span] = value
                s2[i, :, span] = value.astype(BF)
                return 0

            lax.fori_loop(0, n2, add, 0)
            for k in range(1, n2):
                two(k, False).start()

        def finish():
            for k in range(1, n2):
                two(k, True).wait_recv()
            value = s2f[p2, :, span]
            for k in range(1, n2):
                value = value + r2[lax.rem(p2 + k, n2), :, span].astype(F32)
            gh_ref[:, span] = value.astype(BF)
            for k in range(1, n1):
                one(k, False).wait_send()
            for k in range(1, n2):
                two(k, False).wait_send()

        return start, middle, finish

    reduce_z, reduce_y = reducer(0, True), reducer(0, False)
    reduce_1 = reducer(1, False)

    def phase(half, i):
        if half == 0:
            pl.when(c == 0)(reduce_z[i])
            pl.when(c == 1)(reduce_y[i])
        else:
            reduce_1[i]()

    for half in range(2):
        swap[half].wait_recv()
        span = part_of(half)

        def add_pair(i, _):
            yy, zz = i // NZ, lax.rem(i, NZ)
            ssum[yy, zz, :, span] = (graw[yy, zz, c, :, span].astype(F32)
                                     + pair[yy, zz, :, span].astype(F32)).astype(BF)
            return 0
        lax.fori_loop(0, 32, add_pair, 0)
        phase(half, 0)
    for i in range(2):
        for way in range(2):
            g_arrived(way, i)
            g_relay(way, i).start()
    x_sends[2].wait_recv()
    x_sends[3].wait_recv()
    x_relays[0].wait_recv()
    x_relays[1].wait_recv()
    x_fwd = [remote(craw.at[dd, :, :, c], craw.at[dd, :, :, c], xfs.at[i], xfr.at[i], sib)
             for i, dd in enumerate((dl, dr, do))]
    for copy in x_fwd:
        copy.start()
    for i, dd in enumerate((dl, dr, do)):
        remote(craw.at[dd, :, :, 1 - c], craw.at[dd, :, :, 1 - c], xfs.at[i], xfr.at[i],
               sib).wait_recv()
    for dd in (dl, dr, do):
        def flatten_cols(i, _, dd=dd):
            yy, zz = i // 4, lax.rem(i, 4)
            hidc[dd, pl.ds(pl.multiple_of(16 * i, 16), 16), :] = (
                craw[dd, yy, pl.ds(2 * zz, 2)].reshape(16, DC))
            return 0

        lax.fori_loop(0, 16, flatten_cols, 0)
    hidc[d] = hid[:, cols(d)]
    for i in range(2, 4):
        for way in range(2):
            g_arrived(way, i)

    def near(q, _):
        rows = pl.ds(pl.multiple_of(q * 256, 256), 256)
        part = jnp.dot(gt[d, rows], hidc[d], preferred_element_type=F32)
        part = part + jnp.dot(gt[dl, rows], hidc[dl], preferred_element_type=F32)
        part = part + jnp.dot(gt[dr, rows], hidc[dr], preferred_element_type=F32)
        acc[rows, :] = part
        return 0
    lax.fori_loop(0, 4, near, 0)
    phase(0, 1)
    phase(1, 1)

    for i in range(2):
        for way, q in ((0, i), (1, (i + 2) % 4)):
            remote(chunk(do, q), chunk(do, q), gs.at[way, 4 + i], gr.at[way, 4 + i],
                   xdev((dr, dl)[way])).wait_recv()
            rows = pl.ds(q * 256, 256)
            value = jnp.dot(gt[do, rows], hidc[do], preferred_element_type=F32)
            gw_ref[rows, :] = (acc[rows, :] + value).astype(BF)
    phase(0, 2)
    phase(1, 2)
    h_drain()
    t_drain()
    for copy in x_sends + x_relays + x_fwd + g_own + swap:
        copy.wait_send()
    for i in range(2):
        for way in range(2):
            g_relay(way, i).wait_send()
    for k in range(1, 16):
        p = lax.rem(me + k, 16)
        remote(st0, st1.at[me], s1s.at[k], s1r.at[me], dev(y, p // 2, lax.rem(p, 2))).wait_send()
    for k in range(1, NY):
        p = lax.rem(y + k, NY)
        remote(st2s, st2.at[y], s2s.at[k], s2r.at[y], dev(p, z, c)).wait_send()


def shards(hidden, weight, teacher, block_ids):
    vm = pltpu.VMEM
    dma = pltpu.SemaphoreType.DMA
    return pl.pallas_call(
        kernel,
        out_shape=(jax.ShapeDtypeStruct((4, D), BF), jax.ShapeDtypeStruct((V, DC), BF)),
        in_specs=[pl.BlockSpec(memory_space=pl.ANY)] * 3
        + [pl.BlockSpec(memory_space=pltpu.SMEM)],
        out_specs=(pl.BlockSpec(memory_space=vm), pl.BlockSpec(memory_space=vm)),
        scratch_shapes=[
            vm((V, D), BF),
            vm((NY, NZ, 2, 4, D), BF),
            vm((T, D), BF),
            vm((NY, NZ, 2, 2, BLK, BLK), BF),
            vm((NX, NY, NZ, 2, 4, DC), BF),
            vm((NX, T, DC), BF),
            vm((2, 2, NZ, 4, DC), BF),
            vm((V, T), F32),
            vm((NX, V, T), BF),
            vm((T, V), BF),
            vm((NY, NZ, 2, 4, D), BF),
            vm((NY, NZ, 4, D), BF),
            vm((NY, NZ, 4, D), BF),
            vm((32, 4, D), BF),
            vm((8, 4, D), BF),
            vm((8, 4, D), F32),
            vm((8, 4, D), BF),
            vm((4, T), F32),
            vm((16, 4, T), F32),
            vm((4, T), F32),
            vm((NY, 4, T), F32),
            vm((V, DC), F32),
            pltpu.SMEM((16,), jnp.int32),
            dma((3,)),
            dma((2, 4)), dma((2, 4)), dma((32,)), dma((32,)), dma((8,)), dma((8,)),
            dma((2, 4)), dma((2, 4)), dma((32,)), dma((32,)), dma((8,)), dma((8,)),
            dma((6,)), dma((6,)), dma((3,)), dma((3,)),
            dma((16,)), dma((16,)), dma((4,)), dma((4,)),
            dma((2, 6)), dma((2, 6)), dma((2,)), dma((2,)),
            dma((2, 8)), dma((2, 8)), dma((2, 8)), dma((2, 8)),
        ],
        compiler_params=pltpu.CompilerParams(
            collective_id=0, has_side_effects=True, vmem_limit_bytes=60 << 20),
    )(hidden, weight, teacher.reshape(2, BLK, BLK), block_ids)


def solution(mesh):
    placed = (P(("dp", "vocab"), None), P("vocab", None), P("dp", "vocab"), P("dp", None))
    return jax.shard_map(
        shards,
        mesh=mesh,
        in_specs=placed,
        out_specs=(P(("dp", "vocab"), None), P("vocab", "dp")),
        check_vma=False,
    )
```

time: 103 us -> 85.6 us (0.83)
  the two profiles are of different devices: /device:TPU:64 before, /device:TPU:1 now
where the time goes in v2:
time: 85.6 us; the launch traced here: 84.3 us
  Pallas kernels  79.2 us (93%)
  local copies, waits for them, and re-layouts  4.46 us (5%)
    pallas_call x1, Pallas kernels, shards(): pl.pallas_call(kernel, out_shape=(jax.ShapeDtypeStruct((4, D), BF), jax.S...  79.2 us
    unnamed x2, local copies, waits for them, and re-layouts  4.46 us

profile of v2, /device:TPU:1, one launch (start us, length us, event | category | flops | bytes accessed | tf_op | source)
XLA Modules:
  0.0 84.3 jit_solution(4352930086496205163)
XLA Ops:
  0.6 79.2 %shard_map.59 = (bf16[4,4096]{1,0:T(4,128)(2,1)}, bf16[1024,1024]{1,0:T(8,128)(2,1)}) custom-call(bf16[4,4096]{1,0:T(4,128)(2,1)} %hidden_ref.1, bf16[1024,4096]{1,0:T(8,128)(2,1)} %weight_ref.1, bf16[2,128,128]{2,1,0:T(8,128)(2,1)} %bitcast.1, s32[2,64]{1,0:T(2,128)} %ids_ref.1), custom_call_target="tpu_custom_call" | custom-call | tf_op jit(solution)/shard_map/pallas_call | solution.py:460
  79.8 1.4 %copy.8 = bf16[4,4096]{1,0:T(4,128)(2,1)} copy(bf16[4,4096]{1,0:T(4,128)(2,1)} %get-tuple-element.4) | data formatting | bytes 65536
  81.2 3.1 %copy.9 = bf16[1024,1024]{1,0:T(8,128)(2,1)} copy(bf16[1024,1024]{1,0:T(8,128)(2,1)} %get-tuple-element.5) | data formatting | bytes 4194304
